TPU v7x, 32 devices: a whole 2x2x4 slice. The times are simulated.
32 devices in a mesh: groups: 2 (over y), sub: 16 (over z, x, core).
Axes of the slice: x: 2, y: 2, z: 4, core: 2. Of those that a mesh axis runs over, the one named last changes fastest.
Arguments:
- samples: bfloat16 [16896, 512], P(('groups', 'sub')), parts along dimension 0, may hold values from -6 to 6
- channel_order: int32 [512], replicated, may hold values from 0 to 511, each once
- merge_table: int32 [9, 3, 256], replicated, may hold values from 0 to 128, as said below
Outputs:
- spectra: float32 [512, 4096], P(('groups', 'sub')), parts along dimension 0
There are 2 independent parts, one for each index of `groups`. A program takes and returns all parts, laid end to end along the dimension named above; an argument that names none is the same for every part. Nothing has to cross between parts.
Inputs may be any that keep to these rules, and one draw needn't show every extreme that they name: `channel_order`: a permutation of the 512 channels. `merge_table`: for level l, entry j is row d = j % 2**(l-1) of merged subband j // 2**(l-1); with C = max(1, 2**(l-2)) and e = 8, entries 0 and 1 lie in [e * (d // (2 e)), e * (d // (2 e)) + min(C, e)), and entry 2 equals entry 0 or entry 0 plus 1.
All inputs are finite; a program needn't handle non-finite values.
Results may differ from a plain program's by a relative error of at most 0.012.
Values may be sent and summed in bfloat16 or wider, within the bound.
No kernel may reach another device: no remote copies, remote signals or barrier semaphores. Data moves between devices by JAX's collectives and lax.ppermute only.
A program may use at most 64 MiB of HBM per device.

v0:
```python
import math
import jax
import jax.numpy as jnp
from jax import lax
from jax.sharding import PartitionSpec as P

LOCAL = 5
CH_DEV = 32
SAMPLES = 8192


def from_partner(block, axis, apart):
    count = lax.axis_size(axis)
    route = []
    for low in range(count):
        high = low | 1 << apart
        if high != low and high < count:
            route += [(low, high), (high, low)]
    return lax.ppermute(block, axis, route)


def delay_rows(values, shifts, margin, time_axis):
    length = values.shape[time_axis]
    moved = values
    for bit_num in range(max(1, margin.bit_length())):
        offset = 2**bit_num
        rolled = jnp.pad(moved[:, offset:], ((0, 0), (0, offset)))
        flagged = shifts >> bit_num & 1 == 1
        flagged = flagged[:, None]
        moved = jnp.where(flagged, rolled, moved)
    return moved


def merge_level(current, entries, child_rows, span_rows, time_axis):
    outputs = jnp.arange(entries.shape[1], dtype=jnp.int32)
    starts = 2 * child_rows * (outputs // span_rows)
    lower_rows = jnp.take(current, starts + entries[0], axis=1 - time_axis)
    upper_rows = jnp.take(current, starts + child_rows + entries[1], axis=1 - time_axis)
    moved_rows = delay_rows(upper_rows, entries[2], child_rows, time_axis)
    return (lower_rows.astype(jnp.float32) + moved_rows.astype(jnp.float32)).astype(jnp.bfloat16)


def spectrum(delays, channels):
    row_count = delays.shape[0]
    length = delays.shape[1]
    fold_size = length // 128
    first_index = jnp.arange(fold_size, dtype=jnp.int32)
    lane_index = jnp.arange(128, dtype=jnp.int32)
    half_index = jnp.arange(64, dtype=jnp.int32)
    angle_one = (
        2.0
        * math.pi
        / fold_size
        * (first_index[:, None] * first_index[None, :] % fold_size).astype(jnp.float32)
    )
    cos_one = jnp.cos(angle_one).astype(jnp.bfloat16)
    sin_one = jnp.sin(angle_one).astype(jnp.bfloat16)
    angle_two = (
        2.0
        * math.pi
        / length
        * (first_index[:, None] * lane_index[None, :] % length).astype(jnp.float32)
    )
    twist_cos = jnp.cos(angle_two)
    twist_sin = jnp.sin(angle_two)
    angle_three = (
        2.0 * math.pi / 128 * (lane_index[:, None] * half_index[None, :] % 128).astype(jnp.float32)
    )
    cos_three = jnp.cos(angle_three).astype(jnp.bfloat16)
    sin_three = jnp.sin(angle_three).astype(jnp.bfloat16)
    series = delays.reshape(row_count, fold_size, 128)
    first_re = jnp.einsum("kn,rnm->rkm", cos_one, series, preferred_element_type=jnp.float32)
    first_im = -jnp.einsum("kn,rnm->rkm", sin_one, series, preferred_element_type=jnp.float32)
    twisted_re = (first_re * twist_cos + first_im * twist_sin).astype(jnp.bfloat16)
    twisted_im = (first_im * twist_cos - first_re * twist_sin).astype(jnp.bfloat16)
    out_re = jnp.einsum(
        "rkn,nj->rjk", twisted_re, cos_three, preferred_element_type=jnp.float32
    ) + jnp.einsum("rkn,nj->rjk", twisted_im, sin_three, preferred_element_type=jnp.float32)
    out_im = jnp.einsum(
        "rkn,nj->rjk", twisted_im, cos_three, preferred_element_type=jnp.float32
    ) - jnp.einsum("rkn,nj->rjk", twisted_re, sin_three, preferred_element_type=jnp.float32)
    power = (out_re * out_re + out_im * out_im) / (length * channels)
    return power.reshape(row_count, 64 * fold_size)


def local(samples, channel_order, merge_table):
    owners = lax.axis_size("sub")
    owner_index = lax.axis_index("sub")
    owned_rows = CH_DEV // 2
    quarter = CH_DEV // 4
    window = samples.shape[0]
    channels = samples.shape[1]
    ordered = jnp.take(samples, channel_order, axis=1).T.reshape(owners, CH_DEV, window)
    current = lax.all_to_all(ordered, "sub", split_axis=0, concat_axis=2, tiled=True).reshape(
        CH_DEV, window * owners
    )
    for level_num in range(1, LOCAL + 1):
        entries = lax.dynamic_slice_in_dim(
            merge_table[level_num - 1], owner_index * owned_rows, owned_rows, 1
        )
        current = merge_level(
            current, entries, max(1, 2 ** (level_num - 2)), 2 ** (level_num - 1), 1
        )
    block_index = jnp.zeros((), jnp.int32)
    for bit_num in range(owners.bit_length() - 1):
        level_num = LOCAL + bit_num + 1
        half_bit = owner_index >> bit_num & 1
        block_index = block_index * 2 + half_bit
        span_rows = owned_rows * 2 ** (bit_num + 1)
        child_rows = span_rows // 2
        subband = owner_index >> bit_num + 1
        entries = lax.dynamic_slice_in_dim(
            merge_table[level_num - 1],
            subband * span_rows + owned_rows * block_index,
            owned_rows,
            1,
        )
        kept_rows = lax.dynamic_slice_in_dim(current, half_bit * quarter, quarter, 0)
        sent_rows = lax.dynamic_slice_in_dim(current, (1 - half_bit) * quarter, quarter, 0)
        partner = from_partner(sent_rows, "sub", bit_num)
        row_base = quarter * block_index
        is_low = half_bit == 0
        lower_part = jnp.where(is_low, kept_rows, partner)
        upper_part = jnp.where(is_low, partner, kept_rows)
        lower_rows = jnp.take(lower_part, entries[0] - row_base, axis=0)
        upper_rows = jnp.take(upper_part, entries[1] - row_base, axis=0)
        moved_rows = delay_rows(upper_rows, entries[2], child_rows, 1)
        current = (lower_rows.astype(jnp.float32) + moved_rows.astype(jnp.float32)).astype(
            jnp.bfloat16
        )
    return spectrum(current[:, :SAMPLES], channels)


def solution(mesh):
    in_specs = (P(("groups", "sub"), None), P(), P())
    out_specs = P(("groups", "sub"), None)
    return jax.shard_map(local, mesh=mesh, in_specs=in_specs, out_specs=out_specs, check_vma=False)
```

profile of v0, /device:TPU:0, one launch (start us, length us, event | category | flops | bytes accessed | tf_op | source)
XLA Modules:
  0.0 79.7 jit_solution(5246893528105562320)
XLA Ops:
  0.0 0.8 compare_and_fusion.18
  0.8 1.3 %copy.4 = bf16[528,512]{0,1:T(8,128)(2,1)S(1)} copy(bf16[528,512]{1,0:T(8,128)(2,1)} %param.9) | data formatting | bytes 1081344 | tf_op args[0]
  2.1 2.0 %gather_fusion = bf16[512,528]{1,0:T(8,128)(2,1)S(1)} fusion(bf16[528,512]{0,1:T(8,128)(2,1)S(1)} %copy.4, s32[1024]{0:T(1024)S(1)} %pad_clamp_fusion.18), kind=kCustom, calls=%fused_computation.18 | custom fusion | bytes 1083392 | tf_op jit(solution)/shard_map/jit(_take)/gather | solution.py:93
  4.2 1.0 %broadcast_select_fusion = bf16[512,528]{1,0:T(8,128)(2,1)} fusion(bf16[512,528]{1,0:T(8,128)(2,1)S(1)} %gather_fusion, pred[512]{0:T(512)(128)(4,1)S(1)} %compare_and_fusion.18), kind=kLoop, calls=%fused_computation.29 | loop fusion | flops 270336 | bytes 1081856 | tf_op jit(solution)/shard_map/jit(_take)/select_n | solution.py:93
  5.2 7.4 %all-to-all-start = ((bf16[16,32,528]{2,1,0:T(8,128)(2,1)}), bf16[16,32,528]{2,1,0:T(8,128)(2,1)S(1)}, u32[]{:S(2)}, u32[]{:S(2)}) async-start(bf16[16,32,528]{2,1,0:T(8,128)(2,1)} %bitcast.10), calls=%async_computation | async-start | bytes 1310720 | tf_op jit(solution)/shard_map/all_to_all | solution.py:94
  12.6 0.7 copy-done
  14.3 14.9 %all-to-all-done = bf16[16,32,528]{2,1,0:T(8,128)(2,1)S(1)} async-done(((bf16[16,32,528]{2,1,0:T(8,128)(2,1)}), bf16[16,32,528]{2,1,0:T(8,128)(2,1)S(1)}, u32[]{:S(2)}, u32[]{:S(2)}) %all-to-all-start) | async-done | bytes 540704 | tf_op jit(solution)/shard_map/all_to_all | solution.py:94
  30.0 0.7 gather_fusion.2
  30.7 0.7 gather_fusion.1
  34.5 0.7 gather_fusion.5
  36.0 0.7 gather_fusion.8
  38.5 0.7 gather_fusion.10
  39.2 0.7 gather_fusion.9
  41.5 1.2 %collective-permute-done = bf16[8,8448]{1,0:T(8,128)(2,1)S(1)} collective-permute-done((bf16[8,8448]{1,0:T(8,128)(2,1)S(1)}, bf16[8,8448]{1,0:T(8,128)(2,1)S(1)}, u32[]{:S(2)}, u32[]{:S(2)}) %collective-permute-start) | collective-permute-done | bytes 135200 | tf_op jit(solution)/shard_map/ppermute | solution.py:19
  42.7 0.7 gather_fusion.12
  44.8 0.7 gather_fusion.11
  45.8 1.3 %collective-permute-start.1 = (bf16[8,8448]{1,0:T(8,128)(2,1)S(1)}, bf16[8,8448]{1,0:T(8,128)(2,1)S(1)}, u32[]{:S(2)}, u32[]{:S(2)}) collective-permute-start(bf16[8,8448]{1,0:T(8,128)(2,1)S(1)} %constant_dynamic-slice_fusion.5), channel_id=1, source_target_pairs={{0,2},{2,0},{1,3},{3,1},{4,6},{6,4},{5,7},{7,5},{8,10},{10,8},{9,1... | collective-permute-start | bytes 405512 | tf_op jit(solution)/shard_map/ppermute | solution.py:19
  47.1 4.4 %collective-permute-done.1 = bf16[8,8448]{1,0:T(8,128)(2,1)S(1)} collective-permute-done((bf16[8,8448]{1,0:T(8,128)(2,1)S(1)}, bf16[8,8448]{1,0:T(8,128)(2,1)S(1)}, u32[]{:S(2)}, u32[]{:S(2)}) %collective-permute-start.1) | collective-permute-done | bytes 135200 | tf_op jit(solution)/shard_map/ppermute | solution.py:19
  54.9 2.3 %collective-permute-start.2 = (bf16[8,8448]{1,0:T(8,128)(2,1)S(1)}, bf16[8,8448]{1,0:T(8,128)(2,1)S(1)}, u32[]{:S(2)}, u32[]{:S(2)}) collective-permute-start(bf16[8,8448]{1,0:T(8,128)(2,1)S(1)} %constant_dynamic-slice_fusion.3), channel_id=1, source_target_pairs={{0,4},{4,0},{1,5},{5,1},{2,6},{6,2},{3,7},{7,3},{8,12},{12,8},{9,1... | collective-permute-start | bytes 405512 | tf_op jit(solution)/shard_map/ppermute | solution.py:19
  57.2 3.2 %collective-permute-done.2 = bf16[8,8448]{1,0:T(8,128)(2,1)S(1)} collective-permute-done((bf16[8,8448]{1,0:T(8,128)(2,1)S(1)}, bf16[8,8448]{1,0:T(8,128)(2,1)S(1)}, u32[]{:S(2)}, u32[]{:S(2)}) %collective-permute-start.2) | collective-permute-done | bytes 135200 | tf_op jit(solution)/shard_map/ppermute | solution.py:19
  60.5 0.7 gather_fusion.16
  64.3 2.5 %collective-permute-start.3 = (bf16[8,8448]{1,0:T(8,128)(2,1)S(1)}, bf16[8,8448]{1,0:T(8,128)(2,1)S(1)}, u32[]{:S(2)}, u32[]{:S(2)}) collective-permute-start(bf16[8,8448]{1,0:T(8,128)(2,1)S(1)} %constant_dynamic-slice_fusion.1), channel_id=1, source_target_pairs={{0,8},{8,0},{1,9},{9,1},{2,10},{10,2},{3,11},{11,3},{4,12},{12,4},... | collective-permute-start | bytes 405512 | tf_op jit(solution)/shard_map/ppermute | solution.py:19
  67.0 5.6 %collective-permute-done.3 = bf16[8,8448]{1,0:T(8,128)(2,1)S(1)} collective-permute-done((bf16[8,8448]{1,0:T(8,128)(2,1)S(1)}, bf16[8,8448]{1,0:T(8,128)(2,1)S(1)}, u32[]{:S(2)}, u32[]{:S(2)}) %collective-permute-start.3) | collective-permute-done | bytes 135200 | tf_op jit(solution)/shard_map/ppermute | solution.py:19
  78.8 0.9 %reshape.632 = f32[16,4096]{1,0:T(8,128)} reshape(f32[16,64,64]{2,1,0:T(8,128)S(1)} %fusion.5) | data formatting | bytes 524288 | tf_op jit(solution)/shard_map/reshape | solution.py:83
  (155 shorter events, 22.8 us)
Async XLA Ops:
  0.0 0.8 copy-start.1
  5.2 24.0 %all-to-all-start = ((bf16[16,32,528]{2,1,0:T(8,128)(2,1)}), bf16[16,32,528]{2,1,0:T(8,128)(2,1)S(1)}, u32[]{:S(2)}, u32[]{:S(2)}) async-start(bf16[16,32,528]{2,1,0:T(8,128)(2,1)} %bitcast.10), calls=%async_computation | async-start | bytes 1310720 | tf_op jit(solution)/shard_map/all_to_all | solution.py:94
  12.6 0.8 copy-start
  41.2 1.4 %collective-permute-start = (bf16[8,8448]{1,0:T(8,128)(2,1)S(1)}, bf16[8,8448]{1,0:T(8,128)(2,1)S(1)}, u32[]{:S(2)}, u32[]{:S(2)}) collective-permute-start(bf16[8,8448]{1,0:T(8,128)(2,1)S(1)} %constant_dynamic-slice_fusion.7), channel_id=1, source_target_pairs={{0,1},{1,0},{2,3},{3,2},{4,5},{5,4},{6,7},{7,6},{8,9},{9,8},{10,11... | collective-permute-start | bytes 405512 | tf_op jit(solution)/shard_map/ppermute | solution.py:19
  45.8 5.7 %collective-permute-start.1 = (bf16[8,8448]{1,0:T(8,128)(2,1)S(1)}, bf16[8,8448]{1,0:T(8,128)(2,1)S(1)}, u32[]{:S(2)}, u32[]{:S(2)}) collective-permute-start(bf16[8,8448]{1,0:T(8,128)(2,1)S(1)} %constant_dynamic-slice_fusion.5), channel_id=1, source_target_pairs={{0,2},{2,0},{1,3},{3,1},{4,6},{6,4},{5,7},{7,5},{8,10},{10,8},{9,1... | collective-permute-start | bytes 405512 | tf_op jit(solution)/shard_map/ppermute | solution.py:19
  54.9 5.5 %collective-permute-start.2 = (bf16[8,8448]{1,0:T(8,128)(2,1)S(1)}, bf16[8,8448]{1,0:T(8,128)(2,1)S(1)}, u32[]{:S(2)}, u32[]{:S(2)}) collective-permute-start(bf16[8,8448]{1,0:T(8,128)(2,1)S(1)} %constant_dynamic-slice_fusion.3), channel_id=1, source_target_pairs={{0,4},{4,0},{1,5},{5,1},{2,6},{6,2},{3,7},{7,3},{8,12},{12,8},{9,1... | collective-permute-start | bytes 405512 | tf_op jit(solution)/shard_map/ppermute | solution.py:19
  64.3 8.3 %collective-permute-start.3 = (bf16[8,8448]{1,0:T(8,128)(2,1)S(1)}, bf16[8,8448]{1,0:T(8,128)(2,1)S(1)}, u32[]{:S(2)}, u32[]{:S(2)}) collective-permute-start(bf16[8,8448]{1,0:T(8,128)(2,1)S(1)} %constant_dynamic-slice_fusion.1), channel_id=1, source_target_pairs={{0,8},{8,0},{1,9},{9,1},{2,10},{10,2},{3,11},{11,3},{4,12},{12,4},... | collective-permute-start | bytes 405512 | tf_op jit(solution)/shard_map/ppermute | solution.py:19
where the time goes:
time: 80.1 us; the launch traced here: 79.7 us
  waiting for transfers between devices  29.3 us (37%)
  local copies, waits for them, and re-layouts  24.4 us (30%)
  starting transfers between devices  13.7 us (17%)
  other arithmetic  9.1 us (11%)
  matrix products  2.37 us (3%)
  between operations  0.9 us (1%)
    all_to_all x1, waiting for transfers between devices, local(): lax.all_to_all(ordered, 'sub', split_axis=0, concat_axis=2, tiled=True)  14.9 us
    ppermute x4, waiting for transfers between devices, from_partner(): return lax.ppermute(block, axis, route)  14.4 us
    all_to_all x1, starting transfers between devices, local(): lax.all_to_all(ordered, 'sub', split_axis=0, concat_axis=2, tiled=True)  7.39 us
    ppermute x4, starting transfers between devices, from_partner(): return lax.ppermute(block, axis, route)  6.35 us
    slice x37, local copies, waits for them, and re-layouts, delay_rows(): rolled = jnp.pad(moved[:, offset:], ((0, 0), (0, offset)))  4.93 us
    select_n x28, other arithmetic, delay_rows(): moved = jnp.where(flagged, rolled, moved)  3.93 us
    gather x5, local copies, waits for them, and re-layouts, merge_level(): jnp.take(current, starts + child_rows + entries[1], axis=1 - time_axis)  3.6 us
    gather x5, local copies, waits for them, and re-layouts, merge_level(): lower_rows = jnp.take(current, starts + entries[0], axis=1 - time_axis)  3.59 us
  transfers between devices with their start and end apart: 5, of which 5 were waited for; matrix products, arithmetic and copies ran while one was open for 1% of the time, Pallas kernels for 0%

commit v1 on v0

--- a/solution.py
+++ b/solution.py
@@ -91,9 +91,12 @@
     window = samples.shape[0]
     channels = samples.shape[1]
     ordered = jnp.take(samples, channel_order, axis=1).T.reshape(owners, CH_DEV, window)
-    current = lax.all_to_all(ordered, "sub", split_axis=0, concat_axis=2, tiled=True).reshape(
-        CH_DEV, window * owners
-    )
+    current = jnp.concatenate(
+        jax.lax.all_to_all(
+            jnp.stack(jnp.split(ordered, jax.lax.psum(1, "sub"), axis=0), axis=0), "sub", 0, 0
+        ),
+        axis=2,
+    ).reshape(CH_DEV, window * owners)
     for level_num in range(1, LOCAL + 1):
         entries = lax.dynamic_slice_in_dim(
             merge_table[level_num - 1], owner_index * owned_rows, owned_rows, 1

time: 80.1 us -> 90.2 us (1.13)
  local copies, waits for them, and re-layouts: 24.4 us -> 34.7 us
  other arithmetic: 9.1 us -> 8.03 us
    unnamed x6 -> x25, local copies, waits for them, and re-layouts: 2.11 us -> 11.6 us
    another operation x0 -> x2, local copies, waits for them, and re-layouts: none -> 1.26 us  [the longest x1 0.65 us: local(): current = jnp.concatenate(jax.lax.all_to_all(jnp.stack(jnp.split(ordered,...]
    slice x37 -> x38, local copies, waits for them, and re-layouts: 4.93 us -> 4.99 us  [delay_rows(): rolled = jnp.pad(moved[:, offset:], ((0, 0), (0, offset)))]
where the time goes in v1:
time: 90.2 us; the launch traced here: 89.9 us
  local copies, waits for them, and re-layouts  34.7 us (38%)
  waiting for transfers between devices  29.8 us (33%)
  starting transfers between devices  13.9 us (15%)
  other arithmetic  8.03 us (9%)
  matrix products  2.37 us (3%)
  between operations  1.09 us (1%)
    all_to_all x1, waiting for transfers between devices, local(): jax.lax.all_to_all(jnp.stack(jnp.split(ordered, jax.lax.psum(1, 'sub'), a...  15.5 us
    ppermute x4, waiting for transfers between devices, from_partner(): return lax.ppermute(block, axis, route)  14.3 us
    unnamed x25, local copies, waits for them, and re-layouts  11.6 us
    all_to_all x1, starting transfers between devices, local(): jax.lax.all_to_all(jnp.stack(jnp.split(ordered, jax.lax.psum(1, 'sub'), a...  7.52 us
    ppermute x4, starting transfers between devices, from_partner(): return lax.ppermute(block, axis, route)  6.35 us
    slice x38, local copies, waits for them, and re-layouts, delay_rows(): rolled = jnp.pad(moved[:, offset:], ((0, 0), (0, offset)))  4.99 us
    select_n x28, other arithmetic, delay_rows(): moved = jnp.where(flagged, rolled, moved)  3.93 us
    gather x5, local copies, waits for them, and re-layouts, merge_level(): jnp.take(current, starts + child_rows + entries[1], axis=1 - time_axis)  3.6 us
  transfers between devices with their start and end apart: 5, of which 5 were waited for; matrix products, arithmetic and copies ran while one was open for 1% of the time, Pallas kernels for 0%

profile of v1, /device:TPU:0, one launch (start us, length us, event | category | flops | bytes accessed | tf_op | source)
XLA Modules:
  0.0 89.9 jit_solution(11549918489755444453)
XLA Ops:
  0.0 0.8 compare_select_fusion
  0.8 1.3 %copy.5 = bf16[528,512]{0,1:T(8,128)(2,1)S(1)} copy(bf16[528,512]{1,0:T(8,128)(2,1)} %param.9) | data formatting | bytes 1081344 | tf_op args[0]
  2.1 2.0 %gather_fusion = bf16[512,528]{1,0:T(8,128)(2,1)S(1)} fusion(bf16[528,512]{0,1:T(8,128)(2,1)S(1)} %copy.5, s32[1024]{0:T(1024)S(1)} %pad_clamp_fusion.18), kind=kCustom, calls=%fused_computation.18 | custom fusion | bytes 1083392 | tf_op jit(solution)/shard_map/jit(_take)/gather | solution.py:93
  14.2 7.5 %all-to-all-start = ((bf16[16,1,32,528]{3,2,1,0:T(8,128)(2,1)}), bf16[16,1,32,528]{3,2,1,0:T(8,128)(2,1)S(1)}, u32[]{:S(2)}, u32[]{:S(2)}) async-start(bf16[16,1,32,528]{3,2,1,0:T(8,128)(2,1)} %fusion.7), calls=%async_computation | async-start | bytes 1310720 | tf_op jit(solution)/shard_map/all_to_all | solution.py:95
  22.8 15.5 %all-to-all-done = bf16[16,1,32,528]{3,2,1,0:T(8,128)(2,1)S(1)} async-done(((bf16[16,1,32,528]{3,2,1,0:T(8,128)(2,1)}), bf16[16,1,32,528]{3,2,1,0:T(8,128)(2,1)S(1)}, u32[]{:S(2)}, u32[]{:S(2)}) %all-to-all-start) | async-done | bytes 540704 | tf_op jit(solution)/shard_map/all_to_all | solution.py:95
  39.2 0.7 gather_fusion.2
  40.1 0.7 gather_fusion.1
  44.2 0.7 gather_fusion.5
  45.2 0.7 gather_fusion.8
  47.6 0.7 gather_fusion.10
  49.5 0.7 gather_fusion.9
  50.7 1.1 %collective-permute-done = bf16[8,8448]{1,0:T(8,128)(2,1)S(1)} collective-permute-done((bf16[8,8448]{1,0:T(8,128)(2,1)S(1)}, bf16[8,8448]{1,0:T(8,128)(2,1)S(1)}, u32[]{:S(2)}, u32[]{:S(2)}) %collective-permute-start) | collective-permute-done | bytes 135200 | tf_op jit(solution)/shard_map/ppermute | solution.py:19
  51.9 0.7 gather_fusion.12
  54.0 0.7 gather_fusion.11
  54.9 1.3 %collective-permute-start.1 = (bf16[8,8448]{1,0:T(8,128)(2,1)S(1)}, bf16[8,8448]{1,0:T(8,128)(2,1)S(1)}, u32[]{:S(2)}, u32[]{:S(2)}) collective-permute-start(bf16[8,8448]{1,0:T(8,128)(2,1)S(1)} %constant_dynamic-slice_fusion.5), channel_id=1, source_target_pairs={{0,2},{2,0},{1,3},{3,1},{4,6},{6,4},{5,7},{7,5},{8,10},{10,8},{9,1... | collective-permute-start | bytes 405512 | tf_op jit(solution)/shard_map/ppermute | solution.py:19
  56.3 4.4 %collective-permute-done.1 = bf16[8,8448]{1,0:T(8,128)(2,1)S(1)} collective-permute-done((bf16[8,8448]{1,0:T(8,128)(2,1)S(1)}, bf16[8,8448]{1,0:T(8,128)(2,1)S(1)}, u32[]{:S(2)}, u32[]{:S(2)}) %collective-permute-start.1) | collective-permute-done | bytes 135200 | tf_op jit(solution)/shard_map/ppermute | solution.py:19
  63.1 0.7 gather_fusion.13
  64.1 2.3 %collective-permute-start.2 = (bf16[8,8448]{1,0:T(8,128)(2,1)S(1)}, bf16[8,8448]{1,0:T(8,128)(2,1)S(1)}, u32[]{:S(2)}, u32[]{:S(2)}) collective-permute-start(bf16[8,8448]{1,0:T(8,128)(2,1)S(1)} %constant_dynamic-slice_fusion.3), channel_id=1, source_target_pairs={{0,4},{4,0},{1,5},{5,1},{2,6},{6,2},{3,7},{7,3},{8,12},{12,8},{9,1... | collective-permute-start | bytes 405512 | tf_op jit(solution)/shard_map/ppermute | solution.py:19
  66.4 3.2 %collective-permute-done.2 = bf16[8,8448]{1,0:T(8,128)(2,1)S(1)} collective-permute-done((bf16[8,8448]{1,0:T(8,128)(2,1)S(1)}, bf16[8,8448]{1,0:T(8,128)(2,1)S(1)}, u32[]{:S(2)}, u32[]{:S(2)}) %collective-permute-start.2) | collective-permute-done | bytes 135200 | tf_op jit(solution)/shard_map/ppermute | solution.py:19
  69.6 0.7 gather_fusion.16
  72.3 0.7 gather_fusion.15
  73.4 2.5 %collective-permute-start.3 = (bf16[8,8448]{1,0:T(8,128)(2,1)S(1)}, bf16[8,8448]{1,0:T(8,128)(2,1)S(1)}, u32[]{:S(2)}, u32[]{:S(2)}) collective-permute-start(bf16[8,8448]{1,0:T(8,128)(2,1)S(1)} %constant_dynamic-slice_fusion.1), channel_id=1, source_target_pairs={{0,8},{8,0},{1,9},{9,1},{2,10},{10,2},{3,11},{11,3},{4,12},{12,4},... | collective-permute-start | bytes 405512 | tf_op jit(solution)/shard_map/ppermute | solution.py:19
  76.1 5.6 %collective-permute-done.3 = bf16[8,8448]{1,0:T(8,128)(2,1)S(1)} collective-permute-done((bf16[8,8448]{1,0:T(8,128)(2,1)S(1)}, bf16[8,8448]{1,0:T(8,128)(2,1)S(1)}, u32[]{:S(2)}, u32[]{:S(2)}) %collective-permute-start.3) | collective-permute-done | bytes 135200 | tf_op jit(solution)/shard_map/ppermute | solution.py:19
  89.0 0.9 reshape.660
  (174 shorter events, 32.4 us)
Async XLA Ops:
  0.0 0.8 copy-start.3
  14.2 7.5 %copy-start.2 = (s32[9,3,256]{2,1,0:T(4,128)S(1)}, s32[9,3,256]{2,1,0:T(4,128)}, u32[]{:S(2)}) copy-start(s32[9,3,256]{2,1,0:T(4,128)} %param.11) | copy-start | bytes 82948
  14.2 24.1 %all-to-all-start = ((bf16[16,1,32,528]{3,2,1,0:T(8,128)(2,1)}), bf16[16,1,32,528]{3,2,1,0:T(8,128)(2,1)S(1)}, u32[]{:S(2)}, u32[]{:S(2)}) async-start(bf16[16,1,32,528]{3,2,1,0:T(8,128)(2,1)} %fusion.7), calls=%async_computation | async-start | bytes 1310720 | tf_op jit(solution)/shard_map/all_to_all | solution.py:95
  50.4 1.4 %collective-permute-start = (bf16[8,8448]{1,0:T(8,128)(2,1)S(1)}, bf16[8,8448]{1,0:T(8,128)(2,1)S(1)}, u32[]{:S(2)}, u32[]{:S(2)}) collective-permute-start(bf16[8,8448]{1,0:T(8,128)(2,1)S(1)} %constant_dynamic-slice_fusion.7), channel_id=1, source_target_pairs={{0,1},{1,0},{2,3},{3,2},{4,5},{5,4},{6,7},{7,6},{8,9},{9,8},{10,11... | collective-permute-start | bytes 405512 | tf_op jit(solution)/shard_map/ppermute | solution.py:19
  54.9 5.7 %collective-permute-start.1 = (bf16[8,8448]{1,0:T(8,128)(2,1)S(1)}, bf16[8,8448]{1,0:T(8,128)(2,1)S(1)}, u32[]{:S(2)}, u32[]{:S(2)}) collective-permute-start(bf16[8,8448]{1,0:T(8,128)(2,1)S(1)} %constant_dynamic-slice_fusion.5), channel_id=1, source_target_pairs={{0,2},{2,0},{1,3},{3,1},{4,6},{6,4},{5,7},{7,5},{8,10},{10,8},{9,1... | collective-permute-start | bytes 405512 | tf_op jit(solution)/shard_map/ppermute | solution.py:19
  64.1 5.5 %collective-permute-start.2 = (bf16[8,8448]{1,0:T(8,128)(2,1)S(1)}, bf16[8,8448]{1,0:T(8,128)(2,1)S(1)}, u32[]{:S(2)}, u32[]{:S(2)}) collective-permute-start(bf16[8,8448]{1,0:T(8,128)(2,1)S(1)} %constant_dynamic-slice_fusion.3), channel_id=1, source_target_pairs={{0,4},{4,0},{1,5},{5,1},{2,6},{6,2},{3,7},{7,3},{8,12},{12,8},{9,1... | collective-permute-start | bytes 405512 | tf_op jit(solution)/shard_map/ppermute | solution.py:19
  73.4 8.3 %collective-permute-start.3 = (bf16[8,8448]{1,0:T(8,128)(2,1)S(1)}, bf16[8,8448]{1,0:T(8,128)(2,1)S(1)}, u32[]{:S(2)}, u32[]{:S(2)}) collective-permute-start(bf16[8,8448]{1,0:T(8,128)(2,1)S(1)} %constant_dynamic-slice_fusion.1), channel_id=1, source_target_pairs={{0,8},{8,0},{1,9},{9,1},{2,10},{10,2},{3,11},{11,3},{4,12},{12,4},... | collective-permute-start | bytes 405512 | tf_op jit(solution)/shard_map/ppermute | solution.py:19
  84.6 0.7 copy-start
  85.3 1.0 %copy-start.1 = (bf16[16,8448]{1,0:T(8,128)(2,1)S(1)}, bf16[16,8448]{1,0:T(8,128)(2,1)}, u32[]{:S(2)}) copy-start(bf16[16,8448]{1,0:T(8,128)(2,1)} %copy-done) | copy-start | bytes 811012
  85.3 1.0 %slice-start = ((bf16[16,8448]{1,0:T(8,128)(2,1)}), bf16[16,8320]{1,0:T(8,128)(2,1)S(1)}, s32[]{:S(2)}) async-start(bf16[16,8448]{1,0:T(8,128)(2,1)} %copy-done), calls=%async_computation.1 | async-start | bytes 532480 | tf_op jit(solution)/shard_map/slice | solution.py:27
